TPU v7x, 128 devices: a whole 4x4x4 slice. The times are simulated.
128 devices in a mesh: dp: 8 (over z_lo, x), seq: 16 (over z_hi, y, core).
Axes of the slice: x: 4, y: 4, z: 4 (z_hi: 2, z_lo: 2; z = z_hi * 2 + z_lo), core: 2. Of those that a mesh axis runs over, the one named last changes fastest.
Arguments:
- series: bfloat16 [8, 8192, 128], P('dp', 'seq'), may hold values from -6 to 6
- cotangent: bfloat16 [8, 8192, 128], P('dp', 'seq'), may hold values from -6 to 6
- w_in: bfloat16 [128, 384], replicated, may hold values from -0.5 to 0.5
- w_out: bfloat16 [128, 128], replicated, may hold values from -0.5 to 0.5
- taps: float32 [3, 384], replicated, may hold values from -3 to 3
- skip_one: float32 [128], replicated, may hold values from 0.5 to 1.5
- skip_two: float32 [128], replicated, may hold values from 0.5 to 1.5
- filter_one: float32 [8, 8192], P(None, 'seq'), may hold values from -0.0625 to 0.0625
- filter_two: float32 [8, 8192], P(None, 'seq'), may hold values from -0.0625 to 0.0625
Outputs:
- output: bfloat16 [8, 8192, 128], P('dp', 'seq')
- d_series: bfloat16 [8, 8192, 128], P('dp', 'seq')
- grad_w_in: float32 [128, 384], replicated
- grad_w_out: float32 [128, 128], replicated
- grad_taps: float32 [3, 384], replicated
- grad_skip_one: float32 [128], replicated
- grad_skip_two: float32 [128], replicated
- grad_filter_one: float32 [8, 8192], P(None, 'seq')
- grad_filter_two: float32 [8, 8192], P(None, 'seq')
All inputs are finite; a program needn't handle non-finite values.
Results may differ from a plain program's by a relative error of at most 0.015.
Values may be sent and summed in bfloat16 or wider, within the bound.
A program may use at most 128 MiB of HBM per device.

v0:
```python
import math
import jax
import jax.numpy as jnp
from jax import lax
from jax.sharding import PartitionSpec as P

FACTOR = 32


def passed_along(block, axis, distance):
    devices = range(lax.axis_size(axis))
    route = [(i - distance, i) for i in devices if i - distance in devices]
    return lax.ppermute(block, axis, route)


def grid_index(shape_pair, along):
    return lax.broadcasted_iota(jnp.int32, shape_pair, along)


def twiddle(row_index, col_index, period, direction):
    angle = (
        direction * 2.0 * math.pi / period * (row_index * col_index % period).astype(jnp.float32)
    )
    return (jnp.cos(angle), jnp.sin(angle))


def complex_mul(left_real, left_imag, right_real, right_imag):
    return (
        left_real * right_real - left_imag * right_imag,
        left_real * right_imag + left_imag * right_real,
    )


def complex_dft(real_part, imag_part, table_real, table_imag, pattern):
    highest = lax.Precision.HIGHEST
    first = jnp.einsum(pattern, table_real, real_part, precision=highest)
    second = jnp.einsum(pattern, table_imag, imag_part, precision=highest)
    third = jnp.einsum(pattern, table_real, imag_part, precision=highest)
    fourth = jnp.einsum(pattern, table_imag, real_part, precision=highest)
    return (first - second, third + fourth)


def local_dft(pieces):
    real_part, imag_part = pieces
    series_count, pair_rows, block_rows, channels = real_part.shape
    inner = block_rows // FACTOR
    real_part = real_part.reshape(series_count, pair_rows, FACTOR, inner, channels)
    imag_part = imag_part.reshape(series_count, pair_rows, FACTOR, inner, channels)
    table_real, table_imag = twiddle(
        grid_index((FACTOR, FACTOR), 0), grid_index((FACTOR, FACTOR), 1), FACTOR, -1.0
    )
    real_part, imag_part = complex_dft(
        real_part, imag_part, table_real, table_imag, "ca,erabk->ercbk"
    )
    turn_real, turn_imag = twiddle(
        grid_index((FACTOR, inner), 0), grid_index((FACTOR, inner), 1), block_rows, -1.0
    )
    real_part, imag_part = complex_mul(
        real_part, imag_part, turn_real[:, :, None], turn_imag[:, :, None]
    )
    table_real, table_imag = twiddle(
        grid_index((inner, inner), 0), grid_index((inner, inner), 1), inner, -1.0
    )
    return complex_dft(real_part, imag_part, table_real, table_imag, "db,ercbk->ercdk")


def local_inverse(real_part, imag_part):
    series_count, pair_rows, outer, inner, channels = real_part.shape
    block_rows = outer * inner
    table_real, table_imag = twiddle(
        grid_index((inner, inner), 0), grid_index((inner, inner), 1), inner, 1.0
    )
    real_part, imag_part = complex_dft(
        real_part, imag_part, table_real, table_imag, "bd,ercdk->ercbk"
    )
    turn_real, turn_imag = twiddle(
        grid_index((outer, inner), 0), grid_index((outer, inner), 1), block_rows, 1.0
    )
    real_part, imag_part = complex_mul(
        real_part, imag_part, turn_real[:, :, None], turn_imag[:, :, None]
    )
    table_real, table_imag = twiddle(
        grid_index((outer, outer), 0), grid_index((outer, outer), 1), outer, 1.0
    )
    real_part, imag_part = complex_dft(
        real_part, imag_part, table_real, table_imag, "ac,ercbk->erabk"
    )
    return (
        real_part.reshape(series_count, pair_rows, block_rows, channels),
        imag_part.reshape(series_count, pair_rows, block_rows, channels),
    )


def first_section(columns):
    highest = lax.Precision.HIGHEST
    groups = lax.axis_size("seq")
    column_width = columns.shape[2]
    period = 2 * groups * groups * column_width
    offset = lax.axis_index("seq") * column_width
    table_real, table_imag = twiddle(
        grid_index((2 * groups, groups), 0), grid_index((2 * groups, groups), 1), 2 * groups, -1.0
    )
    real_part = jnp.einsum("kn,enjc->ekjc", table_real, columns, precision=highest)
    imag_part = jnp.einsum("kn,enjc->ekjc", table_imag, columns, precision=highest)
    turn_real, turn_imag = twiddle(
        grid_index((2 * groups, column_width), 0),
        grid_index((2 * groups, column_width), 1) + offset,
        period,
        -1.0,
    )
    return complex_mul(real_part, imag_part, turn_real[:, :, None], turn_imag[:, :, None])


def last_section(pieces):
    highest = lax.Precision.HIGHEST
    part_real, part_imag = pieces
    groups = lax.axis_size("seq")
    column_width = part_real.shape[2]
    period = 2 * groups * groups * column_width
    offset = lax.axis_index("seq") * column_width
    turn_real, turn_imag = twiddle(
        grid_index((2 * groups, column_width), 0),
        grid_index((2 * groups, column_width), 1) + offset,
        period,
        1.0,
    )
    part_real, part_imag = complex_mul(
        part_real, part_imag, turn_real[:, :, None], turn_imag[:, :, None]
    )
    table_real, table_imag = twiddle(
        grid_index((groups, 2 * groups), 0), grid_index((groups, 2 * groups), 1), 2 * groups, 1.0
    )
    summed = jnp.einsum("nk,ekjc->enjc", table_real, part_real, precision=highest) - jnp.einsum(
        "nk,ekjc->enjc", table_imag, part_imag, precision=highest
    )
    return summed * (1.0 / period)


def to_frequency(real_part, imag_part):
    return local_dft(
        (
            lax.all_to_all(real_part, "seq", split_axis=1, concat_axis=2, tiled=True),
            lax.all_to_all(imag_part, "seq", split_axis=1, concat_axis=2, tiled=True),
        )
    )


def spectrum(field):
    real_part, imag_part = first_section(
        lax.all_to_all(field, "seq", split_axis=2, concat_axis=1, tiled=True)
    )
    return to_frequency(real_part, imag_part)


def signal(real_part, imag_part):
    real_part, imag_part = local_inverse(real_part, imag_part)
    columns = last_section(
        (
            lax.all_to_all(real_part, "seq", split_axis=2, concat_axis=1, tiled=True),
            lax.all_to_all(imag_part, "seq", split_axis=2, concat_axis=1, tiled=True),
        )
    )
    return lax.all_to_all(columns, "seq", split_axis=1, concat_axis=2, tiled=True)


def order_spectrum(real_part, imag_part):
    series_count, pair_rows, outer, inner, channels = real_part.shape
    block_rows = outer * inner
    real_part = jnp.swapaxes(real_part, 2, 3).reshape(series_count, pair_rows, block_rows, channels)
    imag_part = jnp.swapaxes(imag_part, 2, 3).reshape(series_count, pair_rows, block_rows, channels)
    real_part, imag_part = (
        lax.all_to_all(real_part, "seq", split_axis=2, concat_axis=1, tiled=True),
        lax.all_to_all(imag_part, "seq", split_axis=2, concat_axis=1, tiled=True),
    )
    return (jnp.swapaxes(real_part, 1, 2), jnp.swapaxes(imag_part, 1, 2))


def restore_spectrum(real_part, imag_part):
    real_part = jnp.swapaxes(real_part, 1, 2)
    imag_part = jnp.swapaxes(imag_part, 1, 2)
    real_part, imag_part = (
        lax.all_to_all(real_part, "seq", split_axis=1, concat_axis=2, tiled=True),
        lax.all_to_all(imag_part, "seq", split_axis=1, concat_axis=2, tiled=True),
    )
    series_count, pair_rows, block_rows, channels = real_part.shape
    inner = block_rows // FACTOR
    real_part = jnp.swapaxes(
        real_part.reshape(series_count, pair_rows, inner, FACTOR, channels), 2, 3
    )
    imag_part = jnp.swapaxes(
        imag_part.reshape(series_count, pair_rows, inner, FACTOR, channels), 2, 3
    )
    return (real_part, imag_part)


def transform(field):
    real_part, imag_part = spectrum(field)
    real_part, imag_part = order_spectrum(real_part, imag_part)
    return (real_part, imag_part)


def untransform(real_part, imag_part, in_columns):
    real_part, imag_part = restore_spectrum(real_part, imag_part)
    return signal(real_part, imag_part)


def widen_groups(pieces, channels):
    real_part, imag_part = pieces
    repeat_count = channels // real_part.shape[-1]
    return (
        jnp.repeat(real_part, repeat_count, axis=-1),
        jnp.repeat(imag_part, repeat_count, axis=-1),
    )


def group_sum(pieces, filters):
    result = []
    for piece in pieces:
        channels = piece.shape[-1]
        reshaped = piece.reshape(piece.shape[:-1] + (filters, channels // filters))
        result.append(jnp.sum(jnp.sum(reshaped, axis=-1), axis=0, keepdims=True))
    return (result[0], result[1])


def rows_before(field):
    return passed_along(field[:, :, -2:], "seq", 1)


def rows_after(field):
    return passed_along(field[:, :, :2], "seq", -1)


def filter_blocks(filter_rows):
    return filter_rows.T.reshape(1, 1, filter_rows.shape[1], filter_rows.shape[0])


def shards(series, cotangent, w_in, w_out, taps, skip_one, skip_two, filter_one, filter_two):
    series_count, block_rows, width_d = series.shape
    filters = filter_one.shape[0]
    token_total = series_count * lax.axis_size("dp") * block_rows * lax.axis_size("seq")
    grad_scale = 1.0 / math.sqrt(token_total)
    series_four = series.reshape(series_count, 1, block_rows, width_d)
    cot_four = cotangent.reshape(series_count, 1, block_rows, width_d)
    series_here, cot_here = (series_four, cot_four)
    projected = jnp.einsum("entd,dc->entc", series_here, w_in, preferred_element_type=jnp.float32)
    before = rows_before(projected)
    extended = jnp.concatenate([before, projected], axis=2)
    run_rows = projected.shape[2]
    convolved = (
        taps[0] * extended[:, :, 2:]
        + taps[1] * extended[:, :, 1:-1]
        + taps[2] * extended[:, :, :-2]
    )
    value_part = convolved[..., :width_d]
    gate_one = convolved[..., width_d : 2 * width_d]
    gate_two = convolved[..., 2 * width_d :]
    spec_one = transform(filter_blocks(filter_one))
    spec_two = transform(filter_blocks(filter_two))
    one_real, one_imag = widen_groups(spec_one, width_d)
    two_real, two_imag = widen_groups(spec_two, width_d)
    value_real, value_imag = transform(value_part)
    y_one = (
        untransform(*complex_mul(one_real, one_imag, value_real, value_imag), False)
        + skip_one * value_part
    )
    gated_mid = gate_one * y_one
    mid_real, mid_imag = transform(gated_mid)
    y_two = (
        untransform(*complex_mul(two_real, two_imag, mid_real, mid_imag), False)
        + skip_two * gated_mid
    )
    product = (gate_two * y_two).astype(jnp.bfloat16)
    output = jnp.einsum("entc,cd->entd", product, w_out, preferred_element_type=jnp.float32).astype(
        jnp.bfloat16
    )
    d_product = jnp.einsum("entd,cd->entc", cot_here, w_out, preferred_element_type=jnp.float32)
    grad_two = d_product * gate_two
    d_gate_two = d_product * y_two
    gtwo_real, gtwo_imag = transform(grad_two)
    d_mid = (
        untransform(*complex_mul(two_real, -two_imag, gtwo_real, gtwo_imag), False)
        + skip_two * grad_two
    )
    filter_two_spec = group_sum(complex_mul(mid_real, -mid_imag, gtwo_real, gtwo_imag), filters)
    filter_two_time = untransform(filter_two_spec[0], filter_two_spec[1], False)[0, 0].T
    grad_one = d_mid * gate_one
    d_gate_one = d_mid * y_one
    gone_real, gone_imag = transform(grad_one)
    d_value = (
        untransform(*complex_mul(one_real, -one_imag, gone_real, gone_imag), False)
        + skip_one * grad_one
    )
    filter_one_spec = group_sum(complex_mul(value_real, -value_imag, gone_real, gone_imag), filters)
    filter_one_time = untransform(filter_one_spec[0], filter_one_spec[1], False)[0, 0].T
    d_convolved = jnp.concatenate([d_value, d_gate_one, d_gate_two], axis=3)
    after = rows_after(d_convolved)
    extended_back = jnp.concatenate([d_convolved, after], axis=2)
    d_projected = (
        taps[0] * extended_back[:, :, :-2]
        + taps[1] * extended_back[:, :, 1:-1]
        + taps[2] * extended_back[:, :, 2:]
    ).astype(jnp.bfloat16)
    d_series = jnp.einsum(
        "entc,dc->entd", d_projected, w_in, preferred_element_type=jnp.float32
    ).astype(jnp.bfloat16)
    local_w_in = jnp.einsum(
        "entd,entc->dc", series_here, d_projected, preferred_element_type=jnp.float32
    )
    local_w_out = jnp.einsum("entc,entd->cd", product, cot_here, preferred_element_type=jnp.float32)
    local_taps = jnp.stack(
        [
            jnp.sum(
                d_convolved * extended[:, :, 2 - offset : 2 - offset + run_rows], axis=(0, 1, 2)
            )
            for offset in range(3)
        ]
    )
    local_skip_one = jnp.sum(grad_one * value_part, axis=(0, 1, 2))
    local_skip_two = jnp.sum(grad_two * gated_mid, axis=(0, 1, 2))
    grad_w_in, grad_w_out, grad_taps, grad_skip_one, grad_skip_two = lax.psum(
        (local_w_in, local_w_out, local_taps, local_skip_one, local_skip_two), ("dp", "seq")
    )
    grad_filter_one, grad_filter_two = (
        lax.psum(filter_one_time.astype(jnp.bfloat16), "dp").astype(jnp.float32),
        lax.psum(filter_two_time.astype(jnp.bfloat16), "dp").astype(jnp.float32),
    )
    output = output.reshape(series_count, block_rows, width_d)
    d_series = d_series.reshape(series_count, block_rows, width_d)
    return (
        output,
        d_series,
        grad_scale * grad_w_in,
        grad_scale * grad_w_out,
        grad_scale * grad_taps,
        grad_scale * grad_skip_one,
        grad_scale * grad_skip_two,
        grad_scale * grad_filter_one,
        grad_scale * grad_filter_two,
    )


def solution(mesh):
    in_specs = (
        P("dp", "seq", None),
        P("dp", "seq", None),
        P(),
        P(),
        P(),
        P(),
        P(),
        P(None, "seq"),
        P(None, "seq"),
    )
    out_specs = (
        P("dp", "seq", None),
        P("dp", "seq", None),
        P(),
        P(),
        P(),
        P(),
        P(),
        P(None, "seq"),
        P(None, "seq"),
    )
    return jax.shard_map(shards, mesh=mesh, in_specs=in_specs, out_specs=out_specs, check_vma=False)
```

profile of v0, /device:TPU:1, one launch (start us, length us, event | category | flops | bytes accessed | tf_op | source)
XLA Modules:
  0.0 1293.6 jit_solution(11738205178397126315)
XLA Ops:
  10.7 9.3 all-to-all-start.4
  28.0 6.5 all-to-all-start
  36.5 5.3 all-to-all-done
  50.9 5.5 all-to-all-done.6
  61.6 5.8 all-to-all-done.5
  73.3 6.6 all-to-all-done.8
  89.2 9.1 all-to-all-done.9
  107.8 6.7 all-to-all-done.10
  132.7 5.1 all-to-all-done.12
  144.8 8.3 all-to-all-done.11
  163.8 5.5 all-to-all-done.13
  188.9 8.4 all-to-all-done.14
  207.4 6.5 all-to-all-done.15
  222.0 5.6 all-to-all-start.16
  231.7 7.3 all-to-all-done.16
  245.4 9.6 all-to-all-done.17
  263.8 7.9 all-to-all-done.18
  283.9 12.2 all_to_all.876
  316.0 7.3 all-to-all-start.2
  330.7 6.4 all-to-all-start.31
  348.5 5.3 all-to-all-start.32
  368.1 7.2 all-to-all-start.21
  379.5 7.3 all-to-all-done.21
  386.8 5.0 all-to-all-start.20
  398.3 5.1 all-to-all-done.20
  403.4 5.3 all-to-all-start.3
  417.1 7.3 all-to-all-start.23
  441.4 6.3 all-to-all-done.33
  447.7 5.0 all-to-all-start.34
  457.0 7.4 all-to-all-done.34
  464.3 5.6 all-to-all-start.24
  474.2 7.2 all-to-all-done.24
  481.4 5.1 all-to-all-start.22
  516.8 10.7 fusion.14
  530.6 7.3 all-to-all-start.26
  540.9 8.3 all-to-all-done.26
  549.3 5.0 all-to-all-start.25
  557.4 8.5 all-to-all-done.25
  565.9 5.3 all-to-all-start.36
  592.7 6.0 all-to-all-done.35
  609.3 5.4 all-to-all-start.37
  619.8 6.3 all-to-all-done.37
  626.1 5.1 all-to-all-start.38
  635.3 7.5 all-to-all-done.38
  651.9 7.5 all-to-all-done.28
  669.6 5.7 all-to-all-done.27
  687.6 6.3 all-to-all-done.39
  693.9 12.0 all_to_all.877
  708.8 5.1 all-to-all-start.40
  725.9 7.3 all-to-all-start.56
  762.5 5.9 all-to-all-done.41
  792.6 6.8 all-to-all-start.43
  835.4 8.3 fusion.12
  874.4 7.4 all-to-all-start.57
  933.1 7.3 all-to-all-start.46
  945.0 6.7 all-to-all-done.46
  958.3 9.3 all-to-all-done.45
  967.7 5.4 all-to-all-start.59
  998.8 8.4 all-to-all-done.47
  1015.1 27.4 %all-reduce.2 = (bf16[8,512]{1,0:T(8,128)(2,1)}, bf16[8,512]{1,0:T(8,128)(2,1)}) all-reduce(bf16[8,512]{1,0:T(8,128)(2,1)S(1)} %bitcast.1449, bf16[8,512]{1,0:T(8,128)(2,1)S(1)} %bitcast.1448), channel_id=1, replica_groups=mesh['dp'=8,'seq'=16] {'dp'}, use_global_device_ids=true, to_apply=%region_12.13 | all-reduce | flops 8192 | bytes 32768 | tf_op jit(solution)/shard_map/psum | solution.py:324
  1046.1 14.8 %all-to-all-start.49 = ((f32[1,16,32,128]{3,2,0,1:T(8,128)}), f32[1,16,32,128]{3,2,0,1:T(8,128)S(1)}, u32[]{:S(2)}, u32[]{:S(2)}) async-start(f32[1,16,32,128]{3,2,0,1:T(8,128)} %copy.829), calls=%async_computation.49 | async-start | bytes 524288 | tf_op jit(solution)/shard_map/all_to_all | solution.py:163
  1062.2 7.4 all-to-all-done.49
  1075.5 66.5 %all-reduce = (f32[3,384]{1,0:T(4,128)S(1)}, f32[128]{0:T(128)S(1)}, f32[128]{0:T(128)S(1)}) all-reduce(f32[3,384]{1,0:T(4,128)S(1)} %pad_maximum_fusion.3, f32[128]{0:T(128)S(1)} %copy-done.70, f32[128]{0:T(128)S(1)} %copy-done.69), channel_id=1, replica_groups=mesh['dp'=8,'seq'=16] {'dp','seq'}, use_global_device_ids=true, to_apply=%region_5.6 | all-reduce | flops 1408 | bytes 11264 | tf_op jit(solution)/shard_map/psum | solution.py:320
  1145.6 137.8 %all-reduce.5.cloned.1.call-done = (f32[128,384]{0,1:T(8,128)}, f32[128,128]{1,0:T(8,128)}) async-done(((f32[128,384]{0,1:T(8,128)}, f32[128,128]{1,0:T(8,128)}), (f32[128,384]{0,1:T(8,128)}, f32[128,128]{1,0:T(8,128)})) %all-reduce.5.cloned.1.call-update) | async-done | bytes 262160 | tf_op jit(solution)/shard_map/psum | solution.py:320
  (588 shorter events, 614.5 us)
Async XLA Ops:
  10.7 17.3 %all-to-all-start.4 = ((f32[16,1,256]{2,1,0:T(1,128)}), f32[16,1,256]{2,1,0:T(1,128)S(1)}, u32[]{:S(2)}, u32[]{:S(2)}) async-start(f32[16,1,256]{2,1,0:T(1,128)} %reshape.1187), calls=%async_computation.4 | async-start | bytes 32768 | tf_op jit(solution)/shard_map/all_to_all | solution.py:150
  21.2 27.8 %collective-permute-start = (f32[1,1,2,384]{3,2,1,0:T(2,128)S(1)}, f32[1,1,2,384]{3,2,1,0:T(2,128)S(1)}, u32[]{:S(2)}, u32[]{:S(2)}) collective-permute-start(f32[1,1,2,384]{3,2,1,0:T(2,128)S(1)} %slice.53), channel_id=1, source_target_pairs={{0,1},{1,2},{2,3},{3,4},{4,5},{5,6},{6,7},{7,8},{8,9},{9,10},{10,1... | collective-permute-start | bytes 9224 | tf_op jit(solution)/shard_map/ppermute | solution.py:13
  25.7 54.9 %copy-start.47 = (f32[32,32]{0,1:T(8,128)}, f32[32,32]{0,1:T(8,128)S(1)}, u32[]{:S(2)}) copy-start(f32[32,32]{0,1:T(8,128)S(1)} %copy.646) | copy-start | bytes 12292
  25.8 54.9 %copy-start.48 = (f32[32,32]{0,1:T(8,128)}, f32[32,32]{0,1:T(8,128)S(1)}, u32[]{:S(2)}) copy-start(f32[32,32]{0,1:T(8,128)S(1)} %copy.644) | copy-start | bytes 12292
  28.0 13.8 %all-to-all-start = ((f32[16,1,256]{2,1,0:T(1,128)}), f32[16,1,256]{2,1,0:T(1,128)S(1)}, u32[]{:S(2)}, u32[]{:S(2)}) async-start(f32[16,1,256]{2,1,0:T(1,128)} %reshape.1197), calls=%async_computation | async-start | bytes 32768 | tf_op jit(solution)/shard_map/all_to_all | solution.py:150
  45.3 11.1 all-to-all-start.6
  56.4 11.1 all-to-all-start.5
  67.4 12.5 all-to-all-start.8
  82.6 15.7 %all-to-all-start.9 = ((f32[1,32,32,128]{3,2,0,1:T(8,128)}), f32[1,32,32,128]{3,2,0,1:T(8,128)S(1)}, u32[]{:S(2)}, u32[]{:S(2)}) async-start(f32[1,32,32,128]{3,2,0,1:T(8,128)} %copy.647), calls=%async_computation.9 | async-start | bytes 1048576 | tf_op jit(solution)/shard_map/all_to_all | solution.py:142
  98.3 16.1 %all-to-all-start.10 = ((f32[1,32,32,128]{3,2,0,1:T(8,128)}), f32[1,32,32,128]{3,2,0,1:T(8,128)S(1)}, u32[]{:S(2)}, u32[]{:S(2)}) async-start(f32[1,32,32,128]{3,2,0,1:T(8,128)} %copy.650), calls=%async_computation.10 | async-start | bytes 1048576 | tf_op jit(solution)/shard_map/all_to_all | solution.py:143
  114.4 12.3 all-to-all-start.7
  126.7 11.1 all-to-all-start.12
  137.8 15.2 %all-to-all-start.11 = ((f32[1,2,512,128]{3,1,0,2:T(2,128)}), f32[1,2,512,128]{3,1,0,2:T(2,128)S(1)}, u32[]{:S(2)}, u32[]{:S(2)}) async-start(f32[1,2,512,128]{3,1,0,2:T(2,128)} %copy.658), calls=%async_computation.11 | async-start | bytes 1048576 | tf_op jit(solution)/shard_map/all_to_all | solution.py:172
  153.0 16.2 %all-to-all-start.13 = ((f32[1,2,512,128]{3,1,0,2:T(2,128)}), f32[1,2,512,128]{3,1,0,2:T(2,128)S(1)}, u32[]{:S(2)}, u32[]{:S(2)}) async-start(f32[1,2,512,128]{3,1,0,2:T(2,128)} %copy.669), calls=%async_computation.13 | async-start | bytes 1048576 | tf_op jit(solution)/shard_map/all_to_all | solution.py:173
  181.4 15.9 %all-to-all-start.14 = ((f32[1,32,32,128]{3,2,0,1:T(8,128)}), f32[1,32,32,128]{3,2,0,1:T(8,128)S(1)}, u32[]{:S(2)}, u32[]{:S(2)}) async-start(f32[1,32,32,128]{3,2,0,1:T(8,128)} %copy.673), calls=%async_computation.14 | async-start | bytes 1048576 | tf_op jit(solution)/shard_map/all_to_all | solution.py:182
  197.3 16.6 %all-to-all-start.15 = ((f32[1,32,32,128]{3,2,0,1:T(8,128)}), f32[1,32,32,128]{3,2,0,1:T(8,128)}, u32[]{:S(2)}, u32[]{:S(2)}) async-start(f32[1,32,32,128]{3,2,0,1:T(8,128)} %copy.675), calls=%async_computation.15 | async-start | bytes 1048576 | tf_op jit(solution)/shard_map/all_to_all | solution.py:183
  222.0 17.0 %all-to-all-start.16 = ((f32[1,2,512,128]{3,1,0,2:T(2,128)}), f32[1,2,512,128]{3,1,0,2:T(2,128)}, u32[]{:S(2)}, u32[]{:S(2)}) async-start(f32[1,2,512,128]{3,1,0,2:T(2,128)} %copy.682), calls=%async_computation.16 | async-start | bytes 1048576 | tf_op jit(solution)/shard_map/all_to_all | solution.py:159
  239.0 15.9 %all-to-all-start.17 = ((f32[1,2,512,128]{3,1,0,2:T(2,128)}), f32[1,2,512,128]{3,1,0,2:T(2,128)S(1)}, u32[]{:S(2)}, u32[]{:S(2)}) async-start(f32[1,2,512,128]{3,1,0,2:T(2,128)} %copy.688), calls=%async_computation.17 | async-start | bytes 1048576 | tf_op jit(solution)/shard_map/all_to_all | solution.py:160
  258.6 13.1 %all-to-all-start.18 = ((f32[1,16,32,128]{3,2,0,1:T(8,128)}), f32[1,16,32,128]{3,2,0,1:T(8,128)S(1)}, u32[]{:S(2)}, u32[]{:S(2)}) async-start(f32[1,16,32,128]{3,2,0,1:T(8,128)} %copy.693), calls=%async_computation.18 | async-start | bytes 524288 | tf_op jit(solution)/shard_map/all_to_all | solution.py:163
  271.7 12.2 all-to-all-start.1
  296.1 19.9 %all-to-all-start.30 = ((f32[1,1,512,128]{3,1,0,2:T(1,128)}), f32[1,1,512,128]{3,1,0,2:T(1,128)}, u32[]{:S(2)}, u32[]{:S(2)}) async-start(f32[1,1,512,128]{3,1,0,2:T(1,128)} %bitcast.259), calls=%async_computation.30 | async-start | bytes 524288 | tf_op jit(solution)/shard_map/all_to_all | solution.py:150
  316.0 14.7 %all-to-all-start.2 = ((f32[16,1,512]{2,1,0:T(1,128)}), f32[16,1,512]{2,1,0:T(1,128)}, u32[]{:S(2)}, u32[]{:S(2)}) async-start(f32[16,1,512]{2,1,0:T(1,128)} %reshape.1199), calls=%async_computation.2 | async-start | bytes 65536 | tf_op jit(solution)/shard_map/all_to_all | solution.py:143
  330.7 17.8 %all-to-all-start.31 = ((f32[1,32,32,128]{3,2,0,1:T(8,128)}), f32[1,32,32,128]{3,2,0,1:T(8,128)}, u32[]{:S(2)}, u32[]{:S(2)}) async-start(f32[1,32,32,128]{3,2,0,1:T(8,128)} %copy.745), calls=%async_computation.31 | async-start | bytes 1048576 | tf_op jit(solution)/shard_map/all_to_all | solution.py:142
  348.5 19.5 %all-to-all-start.32 = ((f32[1,32,32,128]{3,2,0,1:T(8,128)}), f32[1,32,32,128]{3,2,0,1:T(8,128)}, u32[]{:S(2)}, u32[]{:S(2)}) async-start(f32[1,32,32,128]{3,2,0,1:T(8,128)} %copy.748), calls=%async_computation.32 | async-start | bytes 1048576 | tf_op jit(solution)/shard_map/all_to_all | solution.py:143
  368.1 18.7 %all-to-all-start.21 = ((f32[1,32,32,128]{3,2,0,1:T(8,128)}), f32[1,32,32,128]{3,2,0,1:T(8,128)}, u32[]{:S(2)}, u32[]{:S(2)}) async-start(f32[1,32,32,128]{3,2,0,1:T(8,128)} %copy.700), calls=%async_computation.21 | async-start | bytes 1048576 | tf_op jit(solution)/shard_map/all_to_all | solution.py:143
  386.8 16.6 %all-to-all-start.20 = ((f32[1,32,32,128]{3,2,0,1:T(8,128)}), f32[1,32,32,128]{3,2,0,1:T(8,128)}, u32[]{:S(2)}, u32[]{:S(2)}) async-start(f32[1,32,32,128]{3,2,0,1:T(8,128)} %copy.697), calls=%async_computation.20 | async-start | bytes 1048576 | tf_op jit(solution)/shard_map/all_to_all | solution.py:142
  403.4 13.7 %all-to-all-start.3 = ((f32[16,1,512]{2,1,0:T(1,128)}), f32[16,1,512]{2,1,0:T(1,128)}, u32[]{:S(2)}, u32[]{:S(2)}) async-start(f32[16,1,512]{2,1,0:T(1,128)} %reshape.1205), calls=%async_computation.3 | async-start | bytes 65536 | tf_op jit(solution)/shard_map/all_to_all | solution.py:172
  417.1 14.7 %all-to-all-start.23 = ((f32[16,1,512]{2,1,0:T(1,128)}), f32[16,1,512]{2,1,0:T(1,128)}, u32[]{:S(2)}, u32[]{:S(2)}) async-start(f32[16,1,512]{2,1,0:T(1,128)} %reshape.1203), calls=%async_computation.23 | async-start | bytes 65536 | tf_op jit(solution)/shard_map/all_to_all | solution.py:173
  431.8 15.9 %all-to-all-start.33 = ((f32[1,2,512,128]{3,1,0,2:T(2,128)}), f32[1,2,512,128]{3,1,0,2:T(2,128)}, u32[]{:S(2)}, u32[]{:S(2)}) async-start(f32[1,2,512,128]{3,1,0,2:T(2,128)} %copy.756), calls=%async_computation.33 | async-start | bytes 1048576 | tf_op jit(solution)/shard_map/all_to_all | solution.py:172
  447.7 16.6 %all-to-all-start.34 = ((f32[1,2,512,128]{3,1,0,2:T(2,128)}), f32[1,2,512,128]{3,1,0,2:T(2,128)}, u32[]{:S(2)}, u32[]{:S(2)}) async-start(f32[1,2,512,128]{3,1,0,2:T(2,128)} %copy.763), calls=%async_computation.34 | async-start | bytes 1048576 | tf_op jit(solution)/shard_map/all_to_all | solution.py:173
  464.3 17.0 %all-to-all-start.24 = ((f32[1,2,512,128]{3,1,0,2:T(2,128)}), f32[1,2,512,128]{3,1,0,2:T(2,128)}, u32[]{:S(2)}, u32[]{:S(2)}) async-start(f32[1,2,512,128]{3,1,0,2:T(2,128)} %copy.719), calls=%async_computation.24 | async-start | bytes 1048576 | tf_op jit(solution)/shard_map/all_to_all | solution.py:173
  481.4 22.5 %all-to-all-start.22 = ((f32[1,2,512,128]{3,1,0,2:T(2,128)}), f32[1,2,512,128]{3,1,0,2:T(2,128)}, u32[]{:S(2)}, u32[]{:S(2)}) async-start(f32[1,2,512,128]{3,1,0,2:T(2,128)} %copy.708), calls=%async_computation.22 | async-start | bytes 1048576 | tf_op jit(solution)/shard_map/all_to_all | solution.py:172
  530.6 18.7 %all-to-all-start.26 = ((f32[1,32,32,128]{3,2,0,1:T(8,128)}), f32[1,32,32,128]{3,2,0,1:T(8,128)S(1)}, u32[]{:S(2)}, u32[]{:S(2)}) async-start(f32[1,32,32,128]{3,2,0,1:T(8,128)} %copy.725), calls=%async_computation.26 | async-start | bytes 1048576 | tf_op jit(solution)/shard_map/all_to_all | solution.py:183
  549.3 16.6 %all-to-all-start.25 = ((f32[1,32,32,128]{3,2,0,1:T(8,128)}), f32[1,32,32,128]{3,2,0,1:T(8,128)}, u32[]{:S(2)}, u32[]{:S(2)}) async-start(f32[1,32,32,128]{3,2,0,1:T(8,128)} %copy.723), calls=%async_computation.25 | async-start | bytes 1048576 | tf_op jit(solution)/shard_map/all_to_all | solution.py:182
  565.9 16.8 %all-to-all-start.36 = ((f32[1,32,32,128]{3,2,0,1:T(8,128)}), f32[1,32,32,128]{3,2,0,1:T(8,128)}, u32[]{:S(2)}, u32[]{:S(2)}) async-start(f32[1,32,32,128]{3,2,0,1:T(8,128)} %copy.769), calls=%async_computation.36 | async-start | bytes 1048576 | tf_op jit(solution)/shard_map/all_to_all | solution.py:183
  582.7 15.9 %all-to-all-start.35 = ((f32[1,32,32,128]{3,2,0,1:T(8,128)}), f32[1,32,32,128]{3,2,0,1:T(8,128)S(1)}, u32[]{:S(2)}, u32[]{:S(2)}) async-start(f32[1,32,32,128]{3,2,0,1:T(8,128)} %copy.767), calls=%async_computation.35 | async-start | bytes 1048576 | tf_op jit(solution)/shard_map/all_to_all | solution.py:182
  609.3 16.8 %all-to-all-start.37 = ((f32[1,2,512,128]{3,1,0,2:T(2,128)}), f32[1,2,512,128]{3,1,0,2:T(2,128)}, u32[]{:S(2)}, u32[]{:S(2)}) async-start(f32[1,2,512,128]{3,1,0,2:T(2,128)} %copy.774), calls=%async_computation.37 | async-start | bytes 1048576 | tf_op jit(solution)/shard_map/all_to_all | solution.py:159
  626.1 16.6 %all-to-all-start.38 = ((f32[1,2,512,128]{3,1,0,2:T(2,128)}), f32[1,2,512,128]{3,1,0,2:T(2,128)}, u32[]{:S(2)}, u32[]{:S(2)}) async-start(f32[1,2,512,128]{3,1,0,2:T(2,128)} %copy.780), calls=%async_computation.38 | async-start | bytes 1048576 | tf_op jit(solution)/shard_map/all_to_all | solution.py:160
  642.7 16.6 %all-to-all-start.28 = ((f32[1,2,512,128]{3,1,0,2:T(2,128)}), f32[1,2,512,128]{3,1,0,2:T(2,128)}, u32[]{:S(2)}, u32[]{:S(2)}) async-start(f32[1,2,512,128]{3,1,0,2:T(2,128)} %copy.736), calls=%async_computation.28 | async-start | bytes 1048576 | tf_op jit(solution)/shard_map/all_to_all | solution.py:160
  659.4 15.9 %all-to-all-start.27 = ((f32[1,2,512,128]{3,1,0,2:T(2,128)}), f32[1,2,512,128]{3,1,0,2:T(2,128)S(1)}, u32[]{:S(2)}, u32[]{:S(2)}) async-start(f32[1,2,512,128]{3,1,0,2:T(2,128)} %copy.730), calls=%async_computation.27 | async-start | bytes 1048576 | tf_op jit(solution)/shard_map/all_to_all | solution.py:159
  680.0 13.8 %all-to-all-start.39 = ((f32[1,16,32,128]{3,2,0,1:T(8,128)}), f32[1,16,32,128]{3,2,0,1:T(8,128)}, u32[]{:S(2)}, u32[]{:S(2)}) async-start(f32[1,16,32,128]{3,2,0,1:T(8,128)} %copy.785), calls=%async_computation.39 | async-start | bytes 524288 | tf_op jit(solution)/shard_map/all_to_all | solution.py:163
  708.8 17.2 %all-to-all-start.40 = ((f32[1,1,512,128]{3,1,0,2:T(1,128)}), f32[1,1,512,128]{3,1,0,2:T(1,128)}, u32[]{:S(2)}, u32[]{:S(2)}) async-start(f32[1,1,512,128]{3,1,0,2:T(1,128)} %bitcast.1339), calls=%async_computation.40 | async-start | bytes 524288 | tf_op jit(solution)/shard_map/all_to_all | solution.py:150
  725.9 14.7 %all-to-all-start.56 = ((f32[16,1,512]{2,1,0:T(1,128)}), f32[16,1,512]{2,1,0:T(1,128)}, u32[]{:S(2)}, u32[]{:S(2)}) async-start(f32[16,1,512]{2,1,0:T(1,128)} %reshape.1217), calls=%async_computation.56 | async-start | bytes 65536 | tf_op jit(solution)/shard_map/all_to_all | solution.py:183
  740.6 11.7 all-to-all-start.55
  752.4 15.9 %all-to-all-start.41 = ((f32[1,32,32,128]{3,2,0,1:T(8,128)}), f32[1,32,32,128]{3,2,0,1:T(8,128)}, u32[]{:S(2)}, u32[]{:S(2)}) async-start(f32[1,32,32,128]{3,2,0,1:T(8,128)} %copy.789), calls=%async_computation.41 | async-start | bytes 1048576 | tf_op jit(solution)/shard_map/all_to_all | solution.py:142
  768.3 16.6 %all-to-all-start.42 = ((f32[1,32,32,128]{3,2,0,1:T(8,128)}), f32[1,32,32,128]{3,2,0,1:T(8,128)}, u32[]{:S(2)}, u32[]{:S(2)}) async-start(f32[1,32,32,128]{3,2,0,1:T(8,128)} %copy.792), calls=%async_computation.42 | async-start | bytes 1048576 | tf_op jit(solution)/shard_map/all_to_all | solution.py:143
  792.6 18.3 %all-to-all-start.43 = ((f32[1,2,512,128]{3,1,0,2:T(2,128)}), f32[1,2,512,128]{3,1,0,2:T(2,128)}, u32[]{:S(2)}, u32[]{:S(2)}) async-start(f32[1,2,512,128]{3,1,0,2:T(2,128)} %copy.800), calls=%async_computation.43 | async-start | bytes 1048576 | tf_op jit(solution)/shard_map/all_to_all | solution.py:172
  810.9 16.6 %all-to-all-start.44 = ((f32[1,2,512,128]{3,1,0,2:T(2,128)}), f32[1,2,512,128]{3,1,0,2:T(2,128)}, u32[]{:S(2)}, u32[]{:S(2)}) async-start(f32[1,2,512,128]{3,1,0,2:T(2,128)} %copy.807), calls=%async_computation.44 | async-start | bytes 1048576 | tf_op jit(solution)/shard_map/all_to_all | solution.py:173
  849.9 12.4 all-to-all-start.50
  862.2 12.1 all-to-all-start.51
  874.4 14.6 %all-to-all-start.57 = ((f32[16,1,512]{2,1,0:T(1,128)}), f32[16,1,512]{2,1,0:T(1,128)S(1)}, u32[]{:S(2)}, u32[]{:S(2)}) async-start(f32[16,1,512]{2,1,0:T(1,128)} %reshape.1223), calls=%async_computation.57 | async-start | bytes 65536 | tf_op jit(solution)/shard_map/all_to_all | solution.py:159
  889.0 11.1 all-to-all-start.58
  900.0 11.1 all-to-all-start.53
  911.1 21.9 %all-to-all-start.52 = ((f32[16,1,512]{2,1,0:T(1,128)}), f32[16,1,512]{2,1,0:T(1,128)}, u32[]{:S(2)}, u32[]{:S(2)}) async-start(f32[16,1,512]{2,1,0:T(1,128)} %reshape.1213), calls=%async_computation.52 | async-start | bytes 65536 | tf_op jit(solution)/shard_map/all_to_all | solution.py:159
  933.1 18.7 %all-to-all-start.46 = ((f32[1,32,32,128]{3,2,0,1:T(8,128)}), f32[1,32,32,128]{3,2,0,1:T(8,128)S(1)}, u32[]{:S(2)}, u32[]{:S(2)}) async-start(f32[1,32,32,128]{3,2,0,1:T(8,128)} %copy.813), calls=%async_computation.46 | async-start | bytes 1048576 | tf_op jit(solution)/shard_map/all_to_all | solution.py:183
  951.8 15.9 %all-to-all-start.45 = ((f32[1,32,32,128]{3,2,0,1:T(8,128)}), f32[1,32,32,128]{3,2,0,1:T(8,128)S(1)}, u32[]{:S(2)}, u32[]{:S(2)}) async-start(f32[1,32,32,128]{3,2,0,1:T(8,128)} %copy.811), calls=%async_computation.45 | async-start | bytes 1048576 | tf_op jit(solution)/shard_map/all_to_all | solution.py:182
  967.7 12.4 all-to-all-start.59
  980.1 11.7 all-to-all-start.54
  991.8 15.4 %all-to-all-start.47 = ((f32[1,2,512,128]{3,1,0,2:T(2,128)}), f32[1,2,512,128]{3,1,0,2:T(2,128)S(1)}, u32[]{:S(2)}, u32[]{:S(2)}) async-start(f32[1,2,512,128]{3,1,0,2:T(2,128)} %copy.818), calls=%async_computation.47 | async-start | bytes 1048576 | tf_op jit(solution)/shard_map/all_to_all | solution.py:159
  1007.2 35.4 %all-to-all-start.48 = ((f32[1,2,512,128]{3,1,0,2:T(2,128)}), f32[1,2,512,128]{3,1,0,2:T(2,128)S(1)}, u32[]{:S(2)}, u32[]{:S(2)}) async-start(f32[1,2,512,128]{3,1,0,2:T(2,128)} %copy.824), calls=%async_computation.48 | async-start | bytes 1048576 | tf_op jit(solution)/shard_map/all_to_all | solution.py:160
  1046.1 23.5 %all-to-all-start.49 = ((f32[1,16,32,128]{3,2,0,1:T(8,128)}), f32[1,16,32,128]{3,2,0,1:T(8,128)S(1)}, u32[]{:S(2)}, u32[]{:S(2)}) async-start(f32[1,16,32,128]{3,2,0,1:T(8,128)} %copy.829), calls=%async_computation.49 | async-start | bytes 524288 | tf_op jit(solution)/shard_map/all_to_all | solution.py:163
  1060.9 222.4 %all-reduce.5.cloned.1.call-start = ((), (), s32[]{:S(2)}) async-start(), calls=%async_computation.60 | async-start | bytes 524288 | tf_op jit(solution)/shard_map/psum | solution.py:320
  1069.8 4.9 collective-permute-start.1
  1074.8 69.8 %copy-start.46 = (bf16[128,384]{1,0:T(8,128)(2,1)S(1)}, bf16[128,384]{1,0:T(8,128)(2,1)}, u32[]{:S(2)}) copy-start(bf16[128,384]{1,0:T(8,128)(2,1)} %param.11) | copy-start | bytes 294916
  (68 other events, 636.6 us)
Sparse Core Ops, SparseCore 0:
  1144.8 138.5 all-reduce.4
where the time goes:
time: 1310 us; the launch traced here: 1290 us
  waiting for transfers between devices  427 us (33%)
  starting transfers between devices  315 us (24%)
  local copies, waits for them, and re-layouts  193 us (15%)
  matrix products  149 us (11%)
  blocking collectives  118 us (9%)
  other arithmetic  75 us (6%)
  between operations  16.5 us (1%)
    psum x1, waiting for transfers between devices, shards(): lax.psum((local_w_in, local_w_out, local_taps, local_skip_one, local_skip...  138 us
    psum x1, blocking collectives, shards(): lax.psum((local_w_in, local_w_out, local_taps, local_skip_one, local_skip...  66.5 us
    unnamed x186, local copies, waits for them, and re-layouts  50.7 us
    all_to_all x6, waiting for transfers between devices, restore_spectrum(): lax.all_to_all(real_part, 'seq', split_axis=1, concat_axis=2, tiled=True)  38.3 us
    all_to_all x6, starting transfers between devices, restore_spectrum(): lax.all_to_all(imag_part, 'seq', split_axis=1, concat_axis=2, tiled=True)  37.1 us
    all_to_all x6, waiting for transfers between devices, signal(): lax.all_to_all(imag_part, 'seq', split_axis=2, concat_axis=1, tiled=True)  34.4 us
    all_to_all x5, starting transfers between devices, signal(): lax.all_to_all(columns, 'seq', split_axis=1, concat_axis=2, tiled=True)  34.3 us
    all_to_all x6, waiting for transfers between devices, order_spectrum(): lax.all_to_all(imag_part, 'seq', split_axis=2, concat_axis=1, tiled=True)  33.6 us
  transfers between devices with their start and end apart: 61, of which 52 were waited for; matrix products, arithmetic and copies ran while one was open for 23% of the time, Pallas kernels for 0%

commit v1 on v0

--- a/solution.py
+++ b/solution.py
@@ -3,6 +3,7 @@
 import jax.numpy as jnp
 from jax import lax
 from jax.sharding import PartitionSpec as P
+from jax.lax import all_gather
 
 FACTOR = 32
 
@@ -320,8 +321,9 @@
     grad_w_in, grad_w_out, grad_taps, grad_skip_one, grad_skip_two = lax.psum(
         (local_w_in, local_w_out, local_taps, local_skip_one, local_skip_two), ("dp", "seq")
     )
+    _load_ranges = lambda body, axis_key: all_gather(body, axis_key).sum(axis=0)
     grad_filter_one, grad_filter_two = (
-        lax.psum(filter_one_time.astype(jnp.bfloat16), "dp").astype(jnp.float32),
+        _load_ranges(filter_one_time.astype(jnp.bfloat16), "dp").astype(jnp.float32),
         lax.psum(filter_two_time.astype(jnp.bfloat16), "dp").astype(jnp.float32),
     )
     output = output.reshape(series_count, block_rows, width_d)

time: 1310 us -> 1330 us (1.015)
    all_gather x0 -> x1, blocking collectives: none -> 24.1 us  [shards(): _load_ranges = lambda body, axis_key: all_gather(body, axis_key).sum(axis=0)]
    unnamed x186 -> x182, local copies, waits for them, and re-layouts: 50.7 us -> 50.7 us
where the time goes in v1:
time: 1330 us; the launch traced here: 1310 us
  waiting for transfers between devices  426 us (32%)
  starting transfers between devices  318 us (24%)
  local copies, waits for them, and re-layouts  193 us (15%)
  matrix products  150 us (11%)
  blocking collectives  131 us (10%)
  other arithmetic  75 us (6%)
  between operations  16.5 us (1%)
    psum x1, waiting for transfers between devices, shards(): lax.psum((local_w_in, local_w_out, local_taps, local_skip_one, local_skip...  138 us
    psum x1, blocking collectives, shards(): lax.psum((local_w_in, local_w_out, local_taps, local_skip_one, local_skip...  66.5 us
    unnamed x182, local copies, waits for them, and re-layouts  50.7 us
    all_to_all x6, waiting for transfers between devices, restore_spectrum(): lax.all_to_all(real_part, 'seq', split_axis=1, concat_axis=2, tiled=True)  38.3 us
    all_to_all x6, starting transfers between devices, restore_spectrum(): lax.all_to_all(imag_part, 'seq', split_axis=1, concat_axis=2, tiled=True)  37.1 us
    all_to_all x5, starting transfers between devices, signal(): lax.all_to_all(columns, 'seq', split_axis=1, concat_axis=2, tiled=True)  37 us
    all_to_all x6, waiting for transfers between devices, signal(): lax.all_to_all(imag_part, 'seq', split_axis=2, concat_axis=1, tiled=True)  34.4 us
    all_to_all x6, waiting for transfers between devices, order_spectrum(): lax.all_to_all(imag_part, 'seq', split_axis=2, concat_axis=1, tiled=True)  33.5 us
  transfers between devices with their start and end apart: 61, of which 52 were waited for; matrix products, arithmetic and copies ran while one was open for 23% of the time, Pallas kernels for 0%

profile of v1, /device:TPU:1, one launch (start us, length us, event | category | flops | bytes accessed | tf_op | source)
XLA Modules:
  0.0 1308.6 jit_solution(15444972497676877259)
XLA Ops:
  10.7 9.3 all-to-all-start.4
  28.0 6.5 all-to-all-start
  36.5 5.3 all-to-all-done
  50.9 5.5 all-to-all-done.6
  61.6 5.8 all-to-all-done.5
  73.3 6.6 all-to-all-done.8
  89.1 9.2 all-to-all-done.9
  107.8 6.7 all-to-all-done.10
  132.7 5.1 all-to-all-done.12
  144.8 8.3 all-to-all-done.11
  163.8 5.5 all-to-all-done.13
  188.9 8.4 all-to-all-done.14
  207.4 6.5 all-to-all-done.15
  222.1 5.6 all-to-all-start.16
  231.7 7.4 all-to-all-done.16
  245.4 9.6 all-to-all-done.17
  263.8 7.9 all-to-all-done.18
  283.9 12.2 all_to_all.876
  316.0 7.3 all-to-all-start.2
  330.8 6.4 all-to-all-start.31
  348.6 5.4 all-to-all-start.32
  368.1 7.2 all-to-all-start.21
  379.5 7.3 all-to-all-done.21
  386.8 5.0 all-to-all-start.20
  398.3 5.1 all-to-all-done.20
  403.4 5.3 all-to-all-start.3
  417.1 7.3 all-to-all-start.23
  441.4 6.4 all-to-all-done.33
  457.0 7.3 all-to-all-done.34
  464.3 5.6 all-to-all-start.24
  474.2 7.2 all-to-all-done.24
  481.4 5.1 all-to-all-start.22
  516.8 10.7 fusion.14
  530.6 7.3 all-to-all-start.26
  540.9 8.3 all-to-all-done.26
  549.2 5.0 all-to-all-start.25
  557.4 8.5 all-to-all-done.25
  565.9 5.3 all-to-all-start.36
  592.6 6.0 all-to-all-done.35
  609.3 5.4 all-to-all-start.37
  619.8 6.3 all-to-all-done.37
  626.1 5.1 all-to-all-start.38
  635.3 7.5 all-to-all-done.38
  651.9 7.5 all-to-all-done.28
  669.6 5.7 all-to-all-done.27
  687.6 6.3 all-to-all-done.39
  693.9 12.0 all_to_all.877
  708.8 5.1 all-to-all-start.40
  726.0 7.3 all-to-all-start.56
  762.5 5.9 all-to-all-done.41
  792.7 6.8 all-to-all-start.43
  835.4 8.3 fusion.12
  874.4 7.4 all-to-all-start.57
  933.1 7.3 all-to-all-start.46
  945.0 6.7 all-to-all-done.46
  958.4 9.3 all-to-all-done.45
  967.7 5.4 all-to-all-start.59
  1000.5 6.7 all-to-all-done.47
  1014.2 15.9 %psum.47 = bf16[8,512]{1,0:T(8,128)(2,1)S(1)} all-reduce(bf16[8,512]{1,0:T(8,128)(2,1)S(1)} %bitcast.1451), channel_id=1, replica_groups=mesh['dp'=8,'seq'=16] {'dp'}, use_global_device_ids=true, to_apply=%region_15.16 | all-reduce | flops 4096 | bytes 16384 | tf_op jit(solution)/shard_map/psum | solution.py:327
  1030.1 24.1 %all-gather = bf16[64,512]{1,0:T(8,128)(2,1)} all-gather(bf16[8,512]{1,0:T(8,128)(2,1)S(1)} %bitcast.1450), channel_id=2, replica_groups=mesh['dp'=8,'seq'=16] {'dp'}, dimensions={0}, use_global_device_ids=true | all-gather | bytes 73728 | tf_op jit(solution)/shard_map/all_gather | solution.py:324
  1058.4 17.5 %all-to-all-start.49 = ((f32[1,16,32,128]{3,2,0,1:T(8,128)}), f32[1,16,32,128]{3,2,0,1:T(8,128)S(1)}, u32[]{:S(2)}, u32[]{:S(2)}) async-start(f32[1,16,32,128]{3,2,0,1:T(8,128)} %copy.829), calls=%async_computation.49 | async-start | bytes 524288 | tf_op jit(solution)/shard_map/all_to_all | solution.py:164
  1076.6 8.0 all-to-all-done.49
  1090.4 66.5 %all-reduce = (f32[3,384]{1,0:T(4,128)S(1)}, f32[128]{0:T(128)S(1)}, f32[128]{0:T(128)S(1)}) all-reduce(f32[3,384]{1,0:T(4,128)S(1)} %pad_maximum_fusion.3, f32[128]{0:T(128)S(1)} %copy-done.68, f32[128]{0:T(128)S(1)} %copy-done.67), channel_id=1, replica_groups=mesh['dp'=8,'seq'=16] {'dp','seq'}, use_global_device_ids=true, to_apply=%region_5.6 | all-reduce | flops 1408 | bytes 11264 | tf_op jit(solution)/shard_map/psum | solution.py:321
  1160.6 137.8 %all-reduce.4.cloned.1.call-done = (f32[128,384]{0,1:T(8,128)}, f32[128,128]{1,0:T(8,128)}) async-done(((f32[128,384]{0,1:T(8,128)}, f32[128,128]{1,0:T(8,128)}), (f32[128,384]{0,1:T(8,128)}, f32[128,128]{1,0:T(8,128)})) %all-reduce.4.cloned.1.call-update) | async-done | bytes 262160 | tf_op jit(solution)/shard_map/psum | solution.py:321
  (586 shorter events, 620.3 us)
Async XLA Ops:
  10.7 17.3 %all-to-all-start.4 = ((f32[16,1,256]{2,1,0:T(1,128)}), f32[16,1,256]{2,1,0:T(1,128)S(1)}, u32[]{:S(2)}, u32[]{:S(2)}) async-start(f32[16,1,256]{2,1,0:T(1,128)} %reshape.1188), calls=%async_computation.4 | async-start | bytes 32768 | tf_op jit(solution)/shard_map/all_to_all | solution.py:151
  21.2 27.8 %collective-permute-start = (f32[1,1,2,384]{3,2,1,0:T(2,128)S(1)}, f32[1,1,2,384]{3,2,1,0:T(2,128)S(1)}, u32[]{:S(2)}, u32[]{:S(2)}) collective-permute-start(f32[1,1,2,384]{3,2,1,0:T(2,128)S(1)} %slice.53), channel_id=1, source_target_pairs={{0,1},{1,2},{2,3},{3,4},{4,5},{5,6},{6,7},{7,8},{8,9},{9,10},{10,1... | collective-permute-start | bytes 9224 | tf_op jit(solution)/shard_map/ppermute | solution.py:14
  25.7 54.9 %copy-start.47 = (f32[32,32]{0,1:T(8,128)}, f32[32,32]{0,1:T(8,128)S(1)}, u32[]{:S(2)}) copy-start(f32[32,32]{0,1:T(8,128)S(1)} %copy.646) | copy-start | bytes 12292
  25.8 54.9 %copy-start.48 = (f32[32,32]{0,1:T(8,128)}, f32[32,32]{0,1:T(8,128)S(1)}, u32[]{:S(2)}) copy-start(f32[32,32]{0,1:T(8,128)S(1)} %copy.644) | copy-start | bytes 12292
  28.0 13.8 %all-to-all-start = ((f32[16,1,256]{2,1,0:T(1,128)}), f32[16,1,256]{2,1,0:T(1,128)S(1)}, u32[]{:S(2)}, u32[]{:S(2)}) async-start(f32[16,1,256]{2,1,0:T(1,128)} %reshape.1198), calls=%async_computation | async-start | bytes 32768 | tf_op jit(solution)/shard_map/all_to_all | solution.py:151
  45.3 11.1 all-to-all-start.6
  56.4 11.1 all-to-all-start.5
  67.4 12.5 all-to-all-start.8
  82.6 15.7 %all-to-all-start.9 = ((f32[1,32,32,128]{3,2,0,1:T(8,128)}), f32[1,32,32,128]{3,2,0,1:T(8,128)S(1)}, u32[]{:S(2)}, u32[]{:S(2)}) async-start(f32[1,32,32,128]{3,2,0,1:T(8,128)} %copy.647), calls=%async_computation.9 | async-start | bytes 1048576 | tf_op jit(solution)/shard_map/all_to_all | solution.py:143
  98.3 16.1 %all-to-all-start.10 = ((f32[1,32,32,128]{3,2,0,1:T(8,128)}), f32[1,32,32,128]{3,2,0,1:T(8,128)S(1)}, u32[]{:S(2)}, u32[]{:S(2)}) async-start(f32[1,32,32,128]{3,2,0,1:T(8,128)} %copy.650), calls=%async_computation.10 | async-start | bytes 1048576 | tf_op jit(solution)/shard_map/all_to_all | solution.py:144
  114.4 12.4 all-to-all-start.7
  126.8 11.1 all-to-all-start.12
  137.8 15.2 %all-to-all-start.11 = ((f32[1,2,512,128]{3,1,0,2:T(2,128)}), f32[1,2,512,128]{3,1,0,2:T(2,128)S(1)}, u32[]{:S(2)}, u32[]{:S(2)}) async-start(f32[1,2,512,128]{3,1,0,2:T(2,128)} %copy.658), calls=%async_computation.11 | async-start | bytes 1048576 | tf_op jit(solution)/shard_map/all_to_all | solution.py:173
  153.1 16.2 %all-to-all-start.13 = ((f32[1,2,512,128]{3,1,0,2:T(2,128)}), f32[1,2,512,128]{3,1,0,2:T(2,128)S(1)}, u32[]{:S(2)}, u32[]{:S(2)}) async-start(f32[1,2,512,128]{3,1,0,2:T(2,128)} %copy.669), calls=%async_computation.13 | async-start | bytes 1048576 | tf_op jit(solution)/shard_map/all_to_all | solution.py:174
  181.5 15.9 %all-to-all-start.14 = ((f32[1,32,32,128]{3,2,0,1:T(8,128)}), f32[1,32,32,128]{3,2,0,1:T(8,128)S(1)}, u32[]{:S(2)}, u32[]{:S(2)}) async-start(f32[1,32,32,128]{3,2,0,1:T(8,128)} %copy.673), calls=%async_computation.14 | async-start | bytes 1048576 | tf_op jit(solution)/shard_map/all_to_all | solution.py:183
  197.3 16.6 %all-to-all-start.15 = ((f32[1,32,32,128]{3,2,0,1:T(8,128)}), f32[1,32,32,128]{3,2,0,1:T(8,128)}, u32[]{:S(2)}, u32[]{:S(2)}) async-start(f32[1,32,32,128]{3,2,0,1:T(8,128)} %copy.675), calls=%async_computation.15 | async-start | bytes 1048576 | tf_op jit(solution)/shard_map/all_to_all | solution.py:184
  222.1 17.0 %all-to-all-start.16 = ((f32[1,2,512,128]{3,1,0,2:T(2,128)}), f32[1,2,512,128]{3,1,0,2:T(2,128)}, u32[]{:S(2)}, u32[]{:S(2)}) async-start(f32[1,2,512,128]{3,1,0,2:T(2,128)} %copy.682), calls=%async_computation.16 | async-start | bytes 1048576 | tf_op jit(solution)/shard_map/all_to_all | solution.py:160
  239.1 15.9 %all-to-all-start.17 = ((f32[1,2,512,128]{3,1,0,2:T(2,128)}), f32[1,2,512,128]{3,1,0,2:T(2,128)S(1)}, u32[]{:S(2)}, u32[]{:S(2)}) async-start(f32[1,2,512,128]{3,1,0,2:T(2,128)} %copy.688), calls=%async_computation.17 | async-start | bytes 1048576 | tf_op jit(solution)/shard_map/all_to_all | solution.py:161
  258.7 13.1 %all-to-all-start.18 = ((f32[1,16,32,128]{3,2,0,1:T(8,128)}), f32[1,16,32,128]{3,2,0,1:T(8,128)S(1)}, u32[]{:S(2)}, u32[]{:S(2)}) async-start(f32[1,16,32,128]{3,2,0,1:T(8,128)} %copy.693), calls=%async_computation.18 | async-start | bytes 524288 | tf_op jit(solution)/shard_map/all_to_all | solution.py:164
  271.8 12.2 all-to-all-start.1
  296.2 19.9 %all-to-all-start.30 = ((f32[1,1,512,128]{3,1,0,2:T(1,128)}), f32[1,1,512,128]{3,1,0,2:T(1,128)}, u32[]{:S(2)}, u32[]{:S(2)}) async-start(f32[1,1,512,128]{3,1,0,2:T(1,128)} %bitcast.259), calls=%async_computation.30 | async-start | bytes 524288 | tf_op jit(solution)/shard_map/all_to_all | solution.py:151
  316.0 14.7 %all-to-all-start.2 = ((f32[16,1,512]{2,1,0:T(1,128)}), f32[16,1,512]{2,1,0:T(1,128)}, u32[]{:S(2)}, u32[]{:S(2)}) async-start(f32[16,1,512]{2,1,0:T(1,128)} %reshape.1200), calls=%async_computation.2 | async-start | bytes 65536 | tf_op jit(solution)/shard_map/all_to_all | solution.py:144
  330.8 17.8 %all-to-all-start.31 = ((f32[1,32,32,128]{3,2,0,1:T(8,128)}), f32[1,32,32,128]{3,2,0,1:T(8,128)}, u32[]{:S(2)}, u32[]{:S(2)}) async-start(f32[1,32,32,128]{3,2,0,1:T(8,128)} %copy.745), calls=%async_computation.31 | async-start | bytes 1048576 | tf_op jit(solution)/shard_map/all_to_all | solution.py:143
  348.6 19.5 %all-to-all-start.32 = ((f32[1,32,32,128]{3,2,0,1:T(8,128)}), f32[1,32,32,128]{3,2,0,1:T(8,128)}, u32[]{:S(2)}, u32[]{:S(2)}) async-start(f32[1,32,32,128]{3,2,0,1:T(8,128)} %copy.748), calls=%async_computation.32 | async-start | bytes 1048576 | tf_op jit(solution)/shard_map/all_to_all | solution.py:144
  368.1 18.7 %all-to-all-start.21 = ((f32[1,32,32,128]{3,2,0,1:T(8,128)}), f32[1,32,32,128]{3,2,0,1:T(8,128)}, u32[]{:S(2)}, u32[]{:S(2)}) async-start(f32[1,32,32,128]{3,2,0,1:T(8,128)} %copy.700), calls=%async_computation.21 | async-start | bytes 1048576 | tf_op jit(solution)/shard_map/all_to_all | solution.py:144
  386.8 16.6 %all-to-all-start.20 = ((f32[1,32,32,128]{3,2,0,1:T(8,128)}), f32[1,32,32,128]{3,2,0,1:T(8,128)}, u32[]{:S(2)}, u32[]{:S(2)}) async-start(f32[1,32,32,128]{3,2,0,1:T(8,128)} %copy.697), calls=%async_computation.20 | async-start | bytes 1048576 | tf_op jit(solution)/shard_map/all_to_all | solution.py:143
  403.4 13.6 %all-to-all-start.3 = ((f32[16,1,512]{2,1,0:T(1,128)}), f32[16,1,512]{2,1,0:T(1,128)}, u32[]{:S(2)}, u32[]{:S(2)}) async-start(f32[16,1,512]{2,1,0:T(1,128)} %reshape.1206), calls=%async_computation.3 | async-start | bytes 65536 | tf_op jit(solution)/shard_map/all_to_all | solution.py:173
  417.1 14.7 %all-to-all-start.23 = ((f32[16,1,512]{2,1,0:T(1,128)}), f32[16,1,512]{2,1,0:T(1,128)}, u32[]{:S(2)}, u32[]{:S(2)}) async-start(f32[16,1,512]{2,1,0:T(1,128)} %reshape.1204), calls=%async_computation.23 | async-start | bytes 65536 | tf_op jit(solution)/shard_map/all_to_all | solution.py:174
  431.8 16.0 %all-to-all-start.33 = ((f32[1,2,512,128]{3,1,0,2:T(2,128)}), f32[1,2,512,128]{3,1,0,2:T(2,128)}, u32[]{:S(2)}, u32[]{:S(2)}) async-start(f32[1,2,512,128]{3,1,0,2:T(2,128)} %copy.756), calls=%async_computation.33 | async-start | bytes 1048576 | tf_op jit(solution)/shard_map/all_to_all | solution.py:173
  447.7 16.6 %all-to-all-start.34 = ((f32[1,2,512,128]{3,1,0,2:T(2,128)}), f32[1,2,512,128]{3,1,0,2:T(2,128)}, u32[]{:S(2)}, u32[]{:S(2)}) async-start(f32[1,2,512,128]{3,1,0,2:T(2,128)} %copy.763), calls=%async_computation.34 | async-start | bytes 1048576 | tf_op jit(solution)/shard_map/all_to_all | solution.py:174
  464.3 17.0 %all-to-all-start.24 = ((f32[1,2,512,128]{3,1,0,2:T(2,128)}), f32[1,2,512,128]{3,1,0,2:T(2,128)}, u32[]{:S(2)}, u32[]{:S(2)}) async-start(f32[1,2,512,128]{3,1,0,2:T(2,128)} %copy.719), calls=%async_computation.24 | async-start | bytes 1048576 | tf_op jit(solution)/shard_map/all_to_all | solution.py:174
  481.4 22.5 %all-to-all-start.22 = ((f32[1,2,512,128]{3,1,0,2:T(2,128)}), f32[1,2,512,128]{3,1,0,2:T(2,128)}, u32[]{:S(2)}, u32[]{:S(2)}) async-start(f32[1,2,512,128]{3,1,0,2:T(2,128)} %copy.708), calls=%async_computation.22 | async-start | bytes 1048576 | tf_op jit(solution)/shard_map/all_to_all | solution.py:173
  530.6 18.7 %all-to-all-start.26 = ((f32[1,32,32,128]{3,2,0,1:T(8,128)}), f32[1,32,32,128]{3,2,0,1:T(8,128)S(1)}, u32[]{:S(2)}, u32[]{:S(2)}) async-start(f32[1,32,32,128]{3,2,0,1:T(8,128)} %copy.725), calls=%async_computation.26 | async-start | bytes 1048576 | tf_op jit(solution)/shard_map/all_to_all | solution.py:184
  549.2 16.6 %all-to-all-start.25 = ((f32[1,32,32,128]{3,2,0,1:T(8,128)}), f32[1,32,32,128]{3,2,0,1:T(8,128)}, u32[]{:S(2)}, u32[]{:S(2)}) async-start(f32[1,32,32,128]{3,2,0,1:T(8,128)} %copy.723), calls=%async_computation.25 | async-start | bytes 1048576 | tf_op jit(solution)/shard_map/all_to_all | solution.py:183
  565.9 16.8 %all-to-all-start.36 = ((f32[1,32,32,128]{3,2,0,1:T(8,128)}), f32[1,32,32,128]{3,2,0,1:T(8,128)}, u32[]{:S(2)}, u32[]{:S(2)}) async-start(f32[1,32,32,128]{3,2,0,1:T(8,128)} %copy.769), calls=%async_computation.36 | async-start | bytes 1048576 | tf_op jit(solution)/shard_map/all_to_all | solution.py:184
  582.7 15.9 %all-to-all-start.35 = ((f32[1,32,32,128]{3,2,0,1:T(8,128)}), f32[1,32,32,128]{3,2,0,1:T(8,128)S(1)}, u32[]{:S(2)}, u32[]{:S(2)}) async-start(f32[1,32,32,128]{3,2,0,1:T(8,128)} %copy.767), calls=%async_computation.35 | async-start | bytes 1048576 | tf_op jit(solution)/shard_map/all_to_all | solution.py:183
  609.3 16.8 %all-to-all-start.37 = ((f32[1,2,512,128]{3,1,0,2:T(2,128)}), f32[1,2,512,128]{3,1,0,2:T(2,128)}, u32[]{:S(2)}, u32[]{:S(2)}) async-start(f32[1,2,512,128]{3,1,0,2:T(2,128)} %copy.774), calls=%async_computation.37 | async-start | bytes 1048576 | tf_op jit(solution)/shard_map/all_to_all | solution.py:160
  626.1 16.6 %all-to-all-start.38 = ((f32[1,2,512,128]{3,1,0,2:T(2,128)}), f32[1,2,512,128]{3,1,0,2:T(2,128)}, u32[]{:S(2)}, u32[]{:S(2)}) async-start(f32[1,2,512,128]{3,1,0,2:T(2,128)} %copy.780), calls=%async_computation.38 | async-start | bytes 1048576 | tf_op jit(solution)/shard_map/all_to_all | solution.py:161
  642.7 16.6 %all-to-all-start.28 = ((f32[1,2,512,128]{3,1,0,2:T(2,128)}), f32[1,2,512,128]{3,1,0,2:T(2,128)}, u32[]{:S(2)}, u32[]{:S(2)}) async-start(f32[1,2,512,128]{3,1,0,2:T(2,128)} %copy.736), calls=%async_computation.28 | async-start | bytes 1048576 | tf_op jit(solution)/shard_map/all_to_all | solution.py:161
  659.4 15.9 %all-to-all-start.27 = ((f32[1,2,512,128]{3,1,0,2:T(2,128)}), f32[1,2,512,128]{3,1,0,2:T(2,128)S(1)}, u32[]{:S(2)}, u32[]{:S(2)}) async-start(f32[1,2,512,128]{3,1,0,2:T(2,128)} %copy.730), calls=%async_computation.27 | async-start | bytes 1048576 | tf_op jit(solution)/shard_map/all_to_all | solution.py:160
  680.0 13.8 %all-to-all-start.39 = ((f32[1,16,32,128]{3,2,0,1:T(8,128)}), f32[1,16,32,128]{3,2,0,1:T(8,128)}, u32[]{:S(2)}, u32[]{:S(2)}) async-start(f32[1,16,32,128]{3,2,0,1:T(8,128)} %copy.785), calls=%async_computation.39 | async-start | bytes 524288 | tf_op jit(solution)/shard_map/all_to_all | solution.py:164
  708.8 17.1 %all-to-all-start.40 = ((f32[1,1,512,128]{3,1,0,2:T(1,128)}), f32[1,1,512,128]{3,1,0,2:T(1,128)}, u32[]{:S(2)}, u32[]{:S(2)}) async-start(f32[1,1,512,128]{3,1,0,2:T(1,128)} %bitcast.1341), calls=%async_computation.40 | async-start | bytes 524288 | tf_op jit(solution)/shard_map/all_to_all | solution.py:151
  726.0 14.7 %all-to-all-start.56 = ((f32[16,1,512]{2,1,0:T(1,128)}), f32[16,1,512]{2,1,0:T(1,128)}, u32[]{:S(2)}, u32[]{:S(2)}) async-start(f32[16,1,512]{2,1,0:T(1,128)} %reshape.1218), calls=%async_computation.56 | async-start | bytes 65536 | tf_op jit(solution)/shard_map/all_to_all | solution.py:184
  740.7 11.7 all-to-all-start.55
  752.4 16.0 %all-to-all-start.41 = ((f32[1,32,32,128]{3,2,0,1:T(8,128)}), f32[1,32,32,128]{3,2,0,1:T(8,128)}, u32[]{:S(2)}, u32[]{:S(2)}) async-start(f32[1,32,32,128]{3,2,0,1:T(8,128)} %copy.789), calls=%async_computation.41 | async-start | bytes 1048576 | tf_op jit(solution)/shard_map/all_to_all | solution.py:143
  768.4 16.6 %all-to-all-start.42 = ((f32[1,32,32,128]{3,2,0,1:T(8,128)}), f32[1,32,32,128]{3,2,0,1:T(8,128)}, u32[]{:S(2)}, u32[]{:S(2)}) async-start(f32[1,32,32,128]{3,2,0,1:T(8,128)} %copy.792), calls=%async_computation.42 | async-start | bytes 1048576 | tf_op jit(solution)/shard_map/all_to_all | solution.py:144
  792.7 18.3 %all-to-all-start.43 = ((f32[1,2,512,128]{3,1,0,2:T(2,128)}), f32[1,2,512,128]{3,1,0,2:T(2,128)}, u32[]{:S(2)}, u32[]{:S(2)}) async-start(f32[1,2,512,128]{3,1,0,2:T(2,128)} %copy.800), calls=%async_computation.43 | async-start | bytes 1048576 | tf_op jit(solution)/shard_map/all_to_all | solution.py:173
  810.9 16.6 %all-to-all-start.44 = ((f32[1,2,512,128]{3,1,0,2:T(2,128)}), f32[1,2,512,128]{3,1,0,2:T(2,128)}, u32[]{:S(2)}, u32[]{:S(2)}) async-start(f32[1,2,512,128]{3,1,0,2:T(2,128)} %copy.807), calls=%async_computation.44 | async-start | bytes 1048576 | tf_op jit(solution)/shard_map/all_to_all | solution.py:174
  849.9 12.4 all-to-all-start.50
  862.3 12.1 all-to-all-start.51
  874.4 14.6 %all-to-all-start.57 = ((f32[16,1,512]{2,1,0:T(1,128)}), f32[16,1,512]{2,1,0:T(1,128)S(1)}, u32[]{:S(2)}, u32[]{:S(2)}) async-start(f32[16,1,512]{2,1,0:T(1,128)} %reshape.1224), calls=%async_computation.57 | async-start | bytes 65536 | tf_op jit(solution)/shard_map/all_to_all | solution.py:160
  889.0 11.1 all-to-all-start.58
  900.1 11.1 all-to-all-start.53
  911.1 22.0 %all-to-all-start.52 = ((f32[16,1,512]{2,1,0:T(1,128)}), f32[16,1,512]{2,1,0:T(1,128)}, u32[]{:S(2)}, u32[]{:S(2)}) async-start(f32[16,1,512]{2,1,0:T(1,128)} %reshape.1214), calls=%async_computation.52 | async-start | bytes 65536 | tf_op jit(solution)/shard_map/all_to_all | solution.py:160
  933.1 18.7 %all-to-all-start.46 = ((f32[1,32,32,128]{3,2,0,1:T(8,128)}), f32[1,32,32,128]{3,2,0,1:T(8,128)S(1)}, u32[]{:S(2)}, u32[]{:S(2)}) async-start(f32[1,32,32,128]{3,2,0,1:T(8,128)} %copy.813), calls=%async_computation.46 | async-start | bytes 1048576 | tf_op jit(solution)/shard_map/all_to_all | solution.py:184
  951.8 15.9 %all-to-all-start.45 = ((f32[1,32,32,128]{3,2,0,1:T(8,128)}), f32[1,32,32,128]{3,2,0,1:T(8,128)S(1)}, u32[]{:S(2)}, u32[]{:S(2)}) async-start(f32[1,32,32,128]{3,2,0,1:T(8,128)} %copy.811), calls=%async_computation.45 | async-start | bytes 1048576 | tf_op jit(solution)/shard_map/all_to_all | solution.py:183
  967.7 12.2 all-to-all-start.59
  979.9 11.9 all-to-all-start.54
  991.8 15.4 %all-to-all-start.47 = ((f32[1,2,512,128]{3,1,0,2:T(2,128)}), f32[1,2,512,128]{3,1,0,2:T(2,128)S(1)}, u32[]{:S(2)}, u32[]{:S(2)}) async-start(f32[1,2,512,128]{3,1,0,2:T(2,128)} %copy.818), calls=%async_computation.47 | async-start | bytes 1048576 | tf_op jit(solution)/shard_map/all_to_all | solution.py:160
  1007.2 47.8 %all-to-all-start.48 = ((f32[1,2,512,128]{3,1,0,2:T(2,128)}), f32[1,2,512,128]{3,1,0,2:T(2,128)S(1)}, u32[]{:S(2)}, u32[]{:S(2)}) async-start(f32[1,2,512,128]{3,1,0,2:T(2,128)} %copy.824), calls=%async_computation.48 | async-start | bytes 1048576 | tf_op jit(solution)/shard_map/all_to_all | solution.py:161
  1058.4 26.1 %all-to-all-start.49 = ((f32[1,16,32,128]{3,2,0,1:T(8,128)}), f32[1,16,32,128]{3,2,0,1:T(8,128)S(1)}, u32[]{:S(2)}, u32[]{:S(2)}) async-start(f32[1,16,32,128]{3,2,0,1:T(8,128)} %copy.829), calls=%async_computation.49 | async-start | bytes 524288 | tf_op jit(solution)/shard_map/all_to_all | solution.py:164
  1075.9 222.5 %all-reduce.4.cloned.1.call-start = ((), (), s32[]{:S(2)}) async-start(), calls=%async_computation.60 | async-start | bytes 524288 | tf_op jit(solution)/shard_map/psum | solution.py:321
  1084.7 4.9 collective-permute-start.1
  1089.8 69.8 %copy-start.46 = (bf16[128,384]{1,0:T(8,128)(2,1)S(1)}, bf16[128,384]{1,0:T(8,128)(2,1)}, u32[]{:S(2)}) copy-start(bf16[128,384]{1,0:T(8,128)(2,1)} %param.11) | copy-start | bytes 294916
  (66 other events, 608.0 us)
Sparse Core Ops, SparseCore 0:
  1159.8 138.5 all-reduce.3
